TPU v7x, 256 devices: a whole 4x4x8 slice. The times are simulated.
256 devices in a mesh: segment: 8 (over z), ctx: 16 (over x, y), dp: 2 (over core).
Axes of the slice: x: 4, y: 4, z: 8, core: 2. Of those that a mesh axis runs over, the one named last changes fastest.
Arguments:
- frames_in: bfloat16 [2, 8, 2048, 1536], P('dp', None, 'ctx'), may hold values from -6 to 6
- lengths: int32 [2, 8], P('dp'), may hold values from 512 to 2048, as said below
- depth_kernel: float32 [8, 32, 1536], P('segment'), may hold values from -1 to 1
- batch_gain: float32 [8, 1536], P('segment'), may hold values from 0.25 to 1.75
- batch_bias: float32 [8, 1536], P('segment'), may hold values from -3 to 3
- out_weight: bfloat16 [8, 1536, 1536], P('segment', 'ctx'), may hold values from -0.15625 to 0.15625
Outputs:
- encoded: bfloat16 [2, 8, 2048, 1536], P('dp', 'segment', 'ctx')
Inputs may be any that keep to these rules, and one draw needn't show every extreme that they name: `lengths`: valid frames of each utterance; in every draw some utterance has all 2048 frames.
All inputs are finite; a program needn't handle non-finite values.
Results may differ from a plain program's by a relative error of at most 0.017.
Values may be sent and summed in bfloat16 or wider, within the bound.
No kernel may reach another device: no remote copies, remote signals or barrier semaphores. Data moves between devices by JAX's collectives and lax.ppermute only.
A program may use at most 64 MiB of HBM per device.

v0:
```python
import jax
import jax.numpy as jnp
from jax import lax
from jax.sharding import PartitionSpec as P

EPSILON = 1e-05


def padded_2(block, sides, width):
    for axis, dim in sides:
        count = lax.axis_size(axis)
        forward = [(i, i + 1) for i in range(count - 1)]
        backward = [(target, source) for source, target in forward]
        low = lax.ppermute(
            lax.slice_in_dim(block, block.shape[dim] - width, None, axis=dim), axis, forward
        )
        high = lax.ppermute(lax.slice_in_dim(block, 0, width, axis=dim), axis, backward)
        block = jnp.concatenate([low, block, high], axis=dim)
    return block


def copy_for_each(x, axis):
    size = lax.axis_size(axis)
    return lax.all_to_all(jnp.broadcast_to(x[None], (size, *x.shape)), axis, 0, 0, tiled=True)


def over_copies(x, axis):
    return copy_for_each(x, axis).sum(axis=0)


def together(arrays, axis):
    line, at, gathered = (jnp.concatenate([a.reshape(-1) for a in arrays]), 0, [])
    total = over_copies(line, axis)
    for a in arrays:
        gathered.append(total[at : at + a.size].reshape(a.shape))
        at += a.size
    return tuple(gathered)


def from_behind(value, axis, steps):
    count = lax.axis_size(axis)
    first, last = (max(0, -steps), min(count, count - steps))
    return lax.ppermute(value, axis, [(source, source + steps) for source in range(first, last)])


def split_up(x, dim, size):
    before, after = (x.shape[:dim], x.shape[dim + 1 :])
    return jnp.moveaxis(x.reshape(*before, size, -1, *after), dim, 0)


def sent_and_summed(x, axis, dim):
    size = lax.axis_size(axis)
    pieces = lax.all_to_all(split_up(x, dim, size), axis, 0, 0, tiled=True)
    return jnp.sum(pieces.astype(jnp.float32), axis=0)


def shards(frames_in, lengths, depth_kernel, batch_gain, batch_bias, out_weight):
    segment_count = lax.axis_size("segment")
    segment_index = lax.axis_index("segment")
    micro_total = frames_in.shape[1]
    owned_count = micro_total // segment_count
    frames_dev = frames_in.shape[2]
    model_width = frames_in.shape[3]
    kernel_size = depth_kernel.shape[1]
    rim_width = kernel_size // 2
    frame_index = lax.axis_index("ctx") * frames_dev + jnp.arange(frames_dev, dtype=jnp.int32)
    full_weight = lax.all_gather(out_weight[0], "ctx", axis=0, tiled=True)

    def project(activation):
        return jnp.dot(activation, full_weight, preferred_element_type=jnp.float32)

    def conv_module(inputs, valid):
        widened = inputs.astype(jnp.float32)
        frame_mean = jnp.mean(widened, axis=1, keepdims=True)
        centred = widened - frame_mean
        frame_var = jnp.mean(centred * centred, axis=1, keepdims=True)
        normed = (centred * lax.rsqrt(frame_var + EPSILON) * valid).astype(jnp.bfloat16)
        padded = padded_2(normed, (("ctx", 0),), rim_width)
        mixed = jnp.zeros(widened.shape, jnp.float32)
        for offset in range(kernel_size):
            mixed = (
                mixed
                + padded[offset : offset + frames_dev].astype(jnp.float32) * depth_kernel[0, offset]
            )
        frames_valid = jnp.sum(valid)
        col_sum, col_squares, frames_all = together(
            (jnp.sum(mixed * valid, axis=0), jnp.sum(valid * mixed * mixed, axis=0), frames_valid),
            ("ctx", "dp"),
        )
        chan_mean = col_sum / frames_all
        chan_var = col_squares / frames_all - chan_mean * chan_mean
        spread = mixed - chan_mean
        scaled = spread * lax.rsqrt(chan_var + EPSILON) * batch_gain[0] + batch_bias[0]
        activation = (scaled * jax.nn.sigmoid(scaled) * valid).astype(jnp.bfloat16)
        return (widened + project(activation)).astype(jnp.bfloat16)

    def tick(step_index, pipe_state):
        incoming, results, owned = pipe_state
        step_index = step_index.astype(jnp.int32)
        batch_index = jnp.clip(step_index - segment_index, 0, micro_total - 1)
        fresh = lax.dynamic_index_in_dim(
            frames_in[0], jnp.minimum(step_index, micro_total - 1), 0, keepdims=False
        )
        inputs = jnp.where(segment_index == 0, fresh, incoming)
        utter_len = lax.dynamic_index_in_dim(lengths[0], batch_index, 0, keepdims=False)
        valid = (frame_index < utter_len).astype(jnp.float32)[:, None]
        layer_out = conv_module(inputs, valid)
        finished = (
            (segment_index == segment_count - 1)
            & (step_index >= segment_index)
            & (step_index - segment_index < micro_total)
        )
        old_slot = lax.dynamic_index_in_dim(results, batch_index, 0, keepdims=True)
        new_slot = jnp.where(finished, layer_out[None], old_slot)
        results = lax.dynamic_update_slice_in_dim(results, new_slot, batch_index, 0)
        incoming = from_behind(layer_out, "segment", 1)
        return (incoming, results, owned)

    tick_total = micro_total + segment_count - 1
    start_state = (
        jnp.zeros((frames_dev, model_width), jnp.bfloat16),
        jnp.zeros((micro_total, frames_dev, model_width), jnp.bfloat16),
        jnp.zeros((owned_count, frames_dev, model_width), jnp.bfloat16),
    )
    final_state = lax.fori_loop(0, tick_total, tick, start_state)
    results = final_state[1]
    keep_mine = jnp.where(segment_index == segment_count - 1, results.astype(jnp.float32), 0.0)
    collected = sent_and_summed(keep_mine.astype(jnp.bfloat16), "segment", 0)
    return collected.astype(jnp.bfloat16)[None]


def solution(mesh):
    placed = (
        P("dp", None, "ctx", None),
        P("dp", None),
        P("segment", None, None),
        P("segment", None),
        P("segment", None),
        P("segment", "ctx", None),
    )
    return jax.shard_map(
        shards,
        mesh=mesh,
        in_specs=placed,
        out_specs=P("dp", "segment", "ctx", None),
        check_vma=False,
    )
```

profile of v0, /device:TPU:8, one launch (start us, length us, event | category | flops | bytes accessed | tf_op | source)
XLA Modules:
  0.0 984.7 jit_solution(2059810741843879672)
XLA Ops:
  7.3 64.2 %all-gather.3.cloned.1.call-done = bf16[1,1536,1536]{2,1,0:T(8,128)(2,1)} async-done(((bf16[1,96,1536]{2,1,0:T(8,128)(2,1)}), bf16[1,1536,1536]{2,1,0:T(8,128)(2,1)}) %all-gather.3.cloned.1.call-update) | async-done | bytes 4718608 | tf_op jit(solution)/shard_map/all_gather | solution.py:67
  73.5 812.7 %while.17 = (s32[]{:T(128)}, bf16[128,1536]{1,0:T(8,128)(2,1)S(1)}, bf16[8,128,1536]{2,1,0:T(8,128)(2,1)}, pred[]{:T(512)}, bf16[1,8,128,1536]{3,2,1,0:T(8,128)(...) while((s32[]{:T(128)}, bf16[128,1536]{1,0:T(8,128)(2,1)S(1)}, ...), condition=%wide.region_7.8_spmd.clone, body=%wide.region_0.7_spmd.clone.sunk | while | flops 646947008 | bytes 15609209 | solution.py:125
  99.2 8.5 all-to-all-done
  116.8 9.3 collective-permute-done.2
  151.8 8.5 all-to-all-done
  170.3 9.3 collective-permute-done.2
  205.2 8.5 all-to-all-done
  223.7 9.3 collective-permute-done.2
  277.2 9.3 collective-permute-done.2
  330.7 9.3 collective-permute-done.2
  385.0 9.3 collective-permute-done.2
  439.6 9.3 collective-permute-done.2
  494.3 9.3 collective-permute-done.2
  548.9 9.3 collective-permute-done.2
  583.9 8.5 all-to-all-done
  603.6 9.3 collective-permute-done.2
  638.6 8.5 all-to-all-done
  658.3 9.3 collective-permute-done.2
  712.9 9.3 collective-permute-done.2
  767.6 9.3 collective-permute-done.2
  802.6 8.5 all-to-all-done
  822.3 9.3 collective-permute-done.2
  876.9 9.3 collective-permute-done.2
  888.7 87.9 %all_to_all.18 = bf16[8,1,128,1536]{3,2,1,0:T(8,128)(2,1)S(1)} all-to-all(bf16[8,1,128,1536]{3,2,1,0:T(8,128)(2,1)S(1)} %fusion.49), channel_id=1, replica_groups=mesh['segment'=8,'ctx'=16,'dp'=2] {'segment'}, dimensions={0} | all-to-all | bytes 6291456 | tf_op jit(solution)/shard_map/all_to_all | solution.py:53
  (383 shorter events, 627.2 us)
Async XLA Ops:
  6.5 64.9 %all-gather.3.cloned.1.call-start = ((), (), s32[]{:S(2)}) async-start(), calls=%async_computation.2 | async-start | bytes 5013504 | tf_op jit(solution)/shard_map/all_gather | solution.py:67
  91.2 16.6 %all-to-all-start = ((f32[32,1,3073]{2,1,0:T(1,128)}), f32[32,1,3073]{2,1,0:T(1,128)S(1)}, u32[]{:S(2)}, u32[]{:S(2)}) async-start(f32[32,1,3073]{2,1,0:T(1,128)} %broadcast_in_dim.58), calls=%async_computation | async-start | bytes 819200 | tf_op jit(solution)/shard_map/while/body/eval_jaxpr/all_to_all | solution.py:24
  144.7 15.6 %all-to-all-start = ((f32[32,1,3073]{2,1,0:T(1,128)}), f32[32,1,3073]{2,1,0:T(1,128)S(1)}, u32[]{:S(2)}, u32[]{:S(2)}) async-start(f32[32,1,3073]{2,1,0:T(1,128)} %broadcast_in_dim.58), calls=%async_computation | async-start | bytes 819200 | tf_op jit(solution)/shard_map/while/body/eval_jaxpr/all_to_all | solution.py:24
  198.2 15.6 %all-to-all-start = ((f32[32,1,3073]{2,1,0:T(1,128)}), f32[32,1,3073]{2,1,0:T(1,128)S(1)}, u32[]{:S(2)}, u32[]{:S(2)}) async-start(f32[32,1,3073]{2,1,0:T(1,128)} %broadcast_in_dim.58), calls=%async_computation | async-start | bytes 819200 | tf_op jit(solution)/shard_map/while/body/eval_jaxpr/all_to_all | solution.py:24
  251.6 15.6 %all-to-all-start = ((f32[32,1,3073]{2,1,0:T(1,128)}), f32[32,1,3073]{2,1,0:T(1,128)S(1)}, u32[]{:S(2)}, u32[]{:S(2)}) async-start(f32[32,1,3073]{2,1,0:T(1,128)} %broadcast_in_dim.58), calls=%async_computation | async-start | bytes 819200 | tf_op jit(solution)/shard_map/while/body/eval_jaxpr/all_to_all | solution.py:24
  305.1 15.6 %all-to-all-start = ((f32[32,1,3073]{2,1,0:T(1,128)}), f32[32,1,3073]{2,1,0:T(1,128)S(1)}, u32[]{:S(2)}, u32[]{:S(2)}) async-start(f32[32,1,3073]{2,1,0:T(1,128)} %broadcast_in_dim.58), calls=%async_computation | async-start | bytes 819200 | tf_op jit(solution)/shard_map/while/body/eval_jaxpr/all_to_all | solution.py:24
  358.6 15.6 %all-to-all-start = ((f32[32,1,3073]{2,1,0:T(1,128)}), f32[32,1,3073]{2,1,0:T(1,128)S(1)}, u32[]{:S(2)}, u32[]{:S(2)}) async-start(f32[32,1,3073]{2,1,0:T(1,128)} %broadcast_in_dim.58), calls=%async_computation | async-start | bytes 819200 | tf_op jit(solution)/shard_map/while/body/eval_jaxpr/all_to_all | solution.py:24
  412.9 15.6 %all-to-all-start = ((f32[32,1,3073]{2,1,0:T(1,128)}), f32[32,1,3073]{2,1,0:T(1,128)S(1)}, u32[]{:S(2)}, u32[]{:S(2)}) async-start(f32[32,1,3073]{2,1,0:T(1,128)} %broadcast_in_dim.58), calls=%async_computation | async-start | bytes 819200 | tf_op jit(solution)/shard_map/while/body/eval_jaxpr/all_to_all | solution.py:24
  467.5 15.6 %all-to-all-start = ((f32[32,1,3073]{2,1,0:T(1,128)}), f32[32,1,3073]{2,1,0:T(1,128)S(1)}, u32[]{:S(2)}, u32[]{:S(2)}) async-start(f32[32,1,3073]{2,1,0:T(1,128)} %broadcast_in_dim.58), calls=%async_computation | async-start | bytes 819200 | tf_op jit(solution)/shard_map/while/body/eval_jaxpr/all_to_all | solution.py:24
  488.6 14.9 %collective-permute-start.2 = (bf16[128,1536]{1,0:T(8,128)(2,1)S(1)}, bf16[128,1536]{1,0:T(8,128)(2,1)S(1)}, u32[]{:S(2)}, u32[]{:S(2)}) collective-permute-start(bf16[128,1536]{1,0:T(8,128)(2,1)S(1)} %get-tuple-element.512), channel_id=1, source_target_pairs={{0,32},{32,64},{64,96},{96,128},{128,160},{160,192},{192,224},{1,3... | collective-permute-start | bytes 1179656 | tf_op jit(solution)/shard_map/while/body/eval_jaxpr/ppermute | solution.py:43
  522.2 15.6 %all-to-all-start = ((f32[32,1,3073]{2,1,0:T(1,128)}), f32[32,1,3073]{2,1,0:T(1,128)S(1)}, u32[]{:S(2)}, u32[]{:S(2)}) async-start(f32[32,1,3073]{2,1,0:T(1,128)} %broadcast_in_dim.58), calls=%async_computation | async-start | bytes 819200 | tf_op jit(solution)/shard_map/while/body/eval_jaxpr/all_to_all | solution.py:24
  543.3 14.8 %collective-permute-start.2 = (bf16[128,1536]{1,0:T(8,128)(2,1)S(1)}, bf16[128,1536]{1,0:T(8,128)(2,1)S(1)}, u32[]{:S(2)}, u32[]{:S(2)}) collective-permute-start(bf16[128,1536]{1,0:T(8,128)(2,1)S(1)} %get-tuple-element.512), channel_id=1, source_target_pairs={{0,32},{32,64},{64,96},{96,128},{128,160},{160,192},{192,224},{1,3... | collective-permute-start | bytes 1179656 | tf_op jit(solution)/shard_map/while/body/eval_jaxpr/ppermute | solution.py:43
  576.8 15.6 %all-to-all-start = ((f32[32,1,3073]{2,1,0:T(1,128)}), f32[32,1,3073]{2,1,0:T(1,128)S(1)}, u32[]{:S(2)}, u32[]{:S(2)}) async-start(f32[32,1,3073]{2,1,0:T(1,128)} %broadcast_in_dim.58), calls=%async_computation | async-start | bytes 819200 | tf_op jit(solution)/shard_map/while/body/eval_jaxpr/all_to_all | solution.py:24
  598.0 14.9 %collective-permute-start.2 = (bf16[128,1536]{1,0:T(8,128)(2,1)S(1)}, bf16[128,1536]{1,0:T(8,128)(2,1)S(1)}, u32[]{:S(2)}, u32[]{:S(2)}) collective-permute-start(bf16[128,1536]{1,0:T(8,128)(2,1)S(1)} %get-tuple-element.512), channel_id=1, source_target_pairs={{0,32},{32,64},{64,96},{96,128},{128,160},{160,192},{192,224},{1,3... | collective-permute-start | bytes 1179656 | tf_op jit(solution)/shard_map/while/body/eval_jaxpr/ppermute | solution.py:43
  631.5 15.6 %all-to-all-start = ((f32[32,1,3073]{2,1,0:T(1,128)}), f32[32,1,3073]{2,1,0:T(1,128)S(1)}, u32[]{:S(2)}, u32[]{:S(2)}) async-start(f32[32,1,3073]{2,1,0:T(1,128)} %broadcast_in_dim.58), calls=%async_computation | async-start | bytes 819200 | tf_op jit(solution)/shard_map/while/body/eval_jaxpr/all_to_all | solution.py:24
  652.7 14.9 %collective-permute-start.2 = (bf16[128,1536]{1,0:T(8,128)(2,1)S(1)}, bf16[128,1536]{1,0:T(8,128)(2,1)S(1)}, u32[]{:S(2)}, u32[]{:S(2)}) collective-permute-start(bf16[128,1536]{1,0:T(8,128)(2,1)S(1)} %get-tuple-element.512), channel_id=1, source_target_pairs={{0,32},{32,64},{64,96},{96,128},{128,160},{160,192},{192,224},{1,3... | collective-permute-start | bytes 1179656 | tf_op jit(solution)/shard_map/while/body/eval_jaxpr/ppermute | solution.py:43
  686.2 15.6 %all-to-all-start = ((f32[32,1,3073]{2,1,0:T(1,128)}), f32[32,1,3073]{2,1,0:T(1,128)S(1)}, u32[]{:S(2)}, u32[]{:S(2)}) async-start(f32[32,1,3073]{2,1,0:T(1,128)} %broadcast_in_dim.58), calls=%async_computation | async-start | bytes 819200 | tf_op jit(solution)/shard_map/while/body/eval_jaxpr/all_to_all | solution.py:24
  707.3 14.9 %collective-permute-start.2 = (bf16[128,1536]{1,0:T(8,128)(2,1)S(1)}, bf16[128,1536]{1,0:T(8,128)(2,1)S(1)}, u32[]{:S(2)}, u32[]{:S(2)}) collective-permute-start(bf16[128,1536]{1,0:T(8,128)(2,1)S(1)} %get-tuple-element.512), channel_id=1, source_target_pairs={{0,32},{32,64},{64,96},{96,128},{128,160},{160,192},{192,224},{1,3... | collective-permute-start | bytes 1179656 | tf_op jit(solution)/shard_map/while/body/eval_jaxpr/ppermute | solution.py:43
  740.9 15.6 %all-to-all-start = ((f32[32,1,3073]{2,1,0:T(1,128)}), f32[32,1,3073]{2,1,0:T(1,128)S(1)}, u32[]{:S(2)}, u32[]{:S(2)}) async-start(f32[32,1,3073]{2,1,0:T(1,128)} %broadcast_in_dim.58), calls=%async_computation | async-start | bytes 819200 | tf_op jit(solution)/shard_map/while/body/eval_jaxpr/all_to_all | solution.py:24
  762.0 14.9 %collective-permute-start.2 = (bf16[128,1536]{1,0:T(8,128)(2,1)S(1)}, bf16[128,1536]{1,0:T(8,128)(2,1)S(1)}, u32[]{:S(2)}, u32[]{:S(2)}) collective-permute-start(bf16[128,1536]{1,0:T(8,128)(2,1)S(1)} %get-tuple-element.512), channel_id=1, source_target_pairs={{0,32},{32,64},{64,96},{96,128},{128,160},{160,192},{192,224},{1,3... | collective-permute-start | bytes 1179656 | tf_op jit(solution)/shard_map/while/body/eval_jaxpr/ppermute | solution.py:43
  795.5 15.6 %all-to-all-start = ((f32[32,1,3073]{2,1,0:T(1,128)}), f32[32,1,3073]{2,1,0:T(1,128)S(1)}, u32[]{:S(2)}, u32[]{:S(2)}) async-start(f32[32,1,3073]{2,1,0:T(1,128)} %broadcast_in_dim.58), calls=%async_computation | async-start | bytes 819200 | tf_op jit(solution)/shard_map/while/body/eval_jaxpr/all_to_all | solution.py:24
  816.6 14.9 %collective-permute-start.2 = (bf16[128,1536]{1,0:T(8,128)(2,1)S(1)}, bf16[128,1536]{1,0:T(8,128)(2,1)S(1)}, u32[]{:S(2)}, u32[]{:S(2)}) collective-permute-start(bf16[128,1536]{1,0:T(8,128)(2,1)S(1)} %get-tuple-element.512), channel_id=1, source_target_pairs={{0,32},{32,64},{64,96},{96,128},{128,160},{160,192},{192,224},{1,3... | collective-permute-start | bytes 1179656 | tf_op jit(solution)/shard_map/while/body/eval_jaxpr/ppermute | solution.py:43
  850.2 15.6 %all-to-all-start = ((f32[32,1,3073]{2,1,0:T(1,128)}), f32[32,1,3073]{2,1,0:T(1,128)S(1)}, u32[]{:S(2)}, u32[]{:S(2)}) async-start(f32[32,1,3073]{2,1,0:T(1,128)} %broadcast_in_dim.58), calls=%async_computation | async-start | bytes 819200 | tf_op jit(solution)/shard_map/while/body/eval_jaxpr/all_to_all | solution.py:24
  871.3 14.9 %collective-permute-start.2 = (bf16[128,1536]{1,0:T(8,128)(2,1)S(1)}, bf16[128,1536]{1,0:T(8,128)(2,1)S(1)}, u32[]{:S(2)}, u32[]{:S(2)}) collective-permute-start(bf16[128,1536]{1,0:T(8,128)(2,1)S(1)} %get-tuple-element.512), channel_id=1, source_target_pairs={{0,32},{32,64},{64,96},{96,128},{128,160},{160,192},{192,224},{1,3... | collective-permute-start | bytes 1179656 | tf_op jit(solution)/shard_map/while/body/eval_jaxpr/ppermute | solution.py:43
  (41 other events, 550.3 us)
Sparse Core Ops, SparseCore 0:
  9.8 61.6 all-gather.2
where the time goes:
time: 988 us; the launch traced here: 985 us
  waiting for transfers between devices  377 us (38%)
  starting transfers between devices  270 us (27%)
  other arithmetic  131 us (13%)
  blocking collectives  87.9 us (9%)
  matrix products  61.5 us (6%)
  local copies, waits for them, and re-layouts  42.8 us (4%)
  between operations  13.4 us (1%)
    ppermute x15, waiting for transfers between devices, from_behind(): lax.ppermute(value, axis, [(source, source + steps) for source in range(f...  139 us
    all_to_all x15, waiting for transfers between devices, copy_for_each(): lax.all_to_all(jnp.broadcast_to(x[None], (size, *x.shape)), axis, 0, 0, t...  128 us
    all_to_all x15, starting transfers between devices, copy_for_each(): lax.all_to_all(jnp.broadcast_to(x[None], (size, *x.shape)), axis, 0, 0, t...  105 us
    all_to_all x1, blocking collectives, sent_and_summed(): pieces = lax.all_to_all(split_up(x, dim, size), axis, 0, 0, tiled=True)  87.9 us
    ppermute x15, starting transfers between devices, from_behind(): lax.ppermute(value, axis, [(source, source + steps) for source in range(f...  76.8 us
    all_gather x1, waiting for transfers between devices, shards(): full_weight = lax.all_gather(out_weight[0], 'ctx', axis=0, tiled=True)  64.2 us
    dot_general x15, matrix products, project(): return jnp.dot(activation, full_weight, preferred_element_type=jnp.float32)  61.5 us
    reduce_sum x15, other arithmetic, conv_module(): jnp.sum(mixed * valid, axis=0)  58 us
  transfers between devices with their start and end apart: 61, of which 46 were waited for; matrix products, arithmetic and copies ran while one was open for 1% of the time, Pallas kernels for 0%

commit v1 on v0

v1 whole, which is shorter than its diff:
```python
import jax
import jax.numpy as jnp
from jax import lax
from jax.sharding import PartitionSpec as P

EPSILON = 1e-05


def shards(frames_in, lengths, depth_kernel, batch_gain, batch_bias, out_weight):
    layer_total = lax.axis_size("segment")
    ctx_count = lax.axis_size("ctx")
    segment_index = lax.axis_index("segment")
    ctx_index = lax.axis_index("ctx")
    dp_index = lax.axis_index("dp")
    frames_dev = frames_in.shape[2]
    model_width = frames_in.shape[3]
    kernel_size = depth_kernel.shape[1]
    rim = kernel_size // 2
    half_rows = out_weight.shape[1] // 2
    mine = lax.dynamic_slice_in_dim(out_weight[0], dp_index * half_rows, half_rows, 0)
    weights = lax.all_gather(mine, ("segment", "ctx", "dp"), axis=0, tiled=True)
    weights = weights.reshape(layer_total, model_width, model_width)
    params = jnp.concatenate([depth_kernel[0], batch_gain, batch_bias], axis=0)
    params = lax.all_gather(params, "segment", axis=0)

    both = [(0, 1), (1, 0)]
    mine_len = lax.dynamic_slice_in_dim(lengths[0], segment_index, 1, 0)
    count = (mine_len + lax.ppermute(mine_len, "dp", both)).astype(jnp.float32)
    frame_index = ctx_index * frames_dev + jnp.arange(frames_dev, dtype=jnp.int32)
    valid = (frame_index < mine_len).astype(jnp.float32)[:, None]
    state = lax.dynamic_index_in_dim(frames_in[0], segment_index, 0, keepdims=False)

    forward = [(i, i + 1) for i in range(ctx_count - 1)]
    backward = [(b, a) for a, b in forward]
    for layer in range(layer_total):
        taps = params[layer, :kernel_size]
        gain = params[layer, kernel_size]
        bias = params[layer, kernel_size + 1]
        widened = state.astype(jnp.float32)
        frame_mean = jnp.mean(widened, axis=1, keepdims=True)
        centred = widened - frame_mean
        frame_var = jnp.mean(centred * centred, axis=1, keepdims=True)
        normed = (centred * lax.rsqrt(frame_var + EPSILON) * valid).astype(jnp.bfloat16)
        low = lax.ppermute(normed[frames_dev - rim :], "ctx", forward)
        high = lax.ppermute(normed[:rim], "ctx", backward)
        padded = jnp.concatenate([low, normed, high], axis=0)
        mixed = jnp.zeros(widened.shape, jnp.float32)
        for offset in range(kernel_size):
            mixed = mixed + padded[offset : offset + frames_dev].astype(jnp.float32) * taps[offset]
        masked = mixed * valid
        sums = jnp.stack([jnp.sum(masked, axis=0), jnp.sum(masked * mixed, axis=0)])
        sums = sums + lax.ppermute(sums, "dp", both)
        sums = lax.all_to_all(
            jnp.broadcast_to(sums[None], (ctx_count, *sums.shape)), "ctx", 0, 0, tiled=True
        ).sum(axis=0)
        chan_mean = sums[0] / count
        chan_var = sums[1] / count - chan_mean * chan_mean
        scaled = (mixed - chan_mean) * (lax.rsqrt(chan_var + EPSILON) * gain) + bias
        activation = (scaled * jax.nn.sigmoid(scaled) * valid).astype(jnp.bfloat16)
        product = jnp.dot(activation, weights[layer], preferred_element_type=jnp.float32)
        state = (widened + product).astype(jnp.bfloat16)
    return state[None, None]


def solution(mesh):
    placed = (
        P("dp", None, "ctx", None),
        P("dp", None),
        P("segment", None, None),
        P("segment", None),
        P("segment", None),
        P("segment", "ctx", None),
    )
    return jax.shard_map(
        shards,
        mesh=mesh,
        in_specs=placed,
        out_specs=P("dp", "segment", "ctx", None),
        check_vma=False,
    )
```

time: 988 us -> 474 us (0.48)
  starting transfers between devices: 270 us -> 98.3 us
  waiting for transfers between devices: 377 us -> 216 us
  other arithmetic: 131 us -> 48.5 us
  blocking collectives: 87.9 us -> 30.5 us
  matrix products: 61.5 us -> 27.3 us
    ppermute x45 -> x25, waiting for transfers between devices: 184 us -> 19.3 us  [the longest x8 9.32 us: shards(): sums = sums + lax.ppermute(sums, 'dp', both)]
    ppermute x45 -> x25, starting transfers between devices: 164 us -> 47.9 us  [the longest x8 23.5 us: shards(): high = lax.ppermute(normed[:rim], 'ctx', backward)]
    all_gather x1 -> x2, waiting for transfers between devices: 64.2 us -> 168 us  [the longest x1 135 us: shards(): weights = lax.all_gather(mine, ('segment', 'ctx', 'dp'), axis=0, tiled=True)]
    all_to_all x15 -> x6, waiting for transfers between devices: 128 us -> 29.1 us  [shards(): lax.all_to_all(jnp.broadcast_to(sums[None], (ctx_count, *sums.shape)), 'c...]
    reduce_sum x76 -> x25, other arithmetic: 103 us -> 35.6 us  [the longest x8 31 us: shards(): sums = jnp.stack([jnp.sum(masked, axis=0), jnp.sum(masked * mixed, axis=0)])]
    all_to_all x1 -> x2, blocking collectives: 87.9 us -> 30.5 us  [shards(): lax.all_to_all(jnp.broadcast_to(sums[None], (ctx_count, *sums.shape)), 'c...]
    all_to_all x15 -> x6, starting transfers between devices: 105 us -> 50.4 us  [shards(): lax.all_to_all(jnp.broadcast_to(sums[None], (ctx_count, *sums.shape)), 'c...]
    dot_general x15 -> x8, matrix products: 61.5 us -> 27.3 us  [shards(): jnp.dot(activation, weights[layer], preferred_element_type=jnp.float32)]
  transfers between devices with their start and end apart: 61 -> 33, of which waited for: 46 -> 24; matrix products, arithmetic and copies ran while one was open for 1% -> 8% of each run, Pallas kernels for 0% -> 0%
where the time goes in v1:
time: 474 us; the launch traced here: 469 us
  waiting for transfers between devices  216 us (46%)
  starting transfers between devices  98.3 us (21%)
  other arithmetic  48.5 us (10%)
  local copies, waits for them, and re-layouts  33.1 us (7%)
  blocking collectives  30.5 us (6%)
  matrix products  27.3 us (6%)
  between operations  15.5 us (3%)
    all_gather x1, waiting for transfers between devices, shards(): weights = lax.all_gather(mine, ('segment', 'ctx', 'dp'), axis=0, tiled=True)  135 us
    all_to_all x6, starting transfers between devices, shards(): lax.all_to_all(jnp.broadcast_to(sums[None], (ctx_count, *sums.shape)), 'c...  50.4 us
    all_gather x1, waiting for transfers between devices, shards(): params = lax.all_gather(params, 'segment', axis=0)  32.4 us
    reduce_sum x8, other arithmetic, shards(): sums = jnp.stack([jnp.sum(masked, axis=0), jnp.sum(masked * mixed, axis=0)])  31 us
    all_to_all x2, blocking collectives, shards(): lax.all_to_all(jnp.broadcast_to(sums[None], (ctx_count, *sums.shape)), 'c...  30.5 us
    all_to_all x6, waiting for transfers between devices, shards(): lax.all_to_all(jnp.broadcast_to(sums[None], (ctx_count, *sums.shape)), 'c...  29.1 us
    dot_general x8, matrix products, shards(): jnp.dot(activation, weights[layer], preferred_element_type=jnp.float32)  27.3 us
    slice x14, local copies, waits for them, and re-layouts, shards(): taps[offset]  24.7 us
  transfers between devices with their start and end apart: 33, of which 24 were waited for; matrix products, arithmetic and copies ran while one was open for 8% of the time, Pallas kernels for 0%

profile of v1, /device:TPU:8, one launch (start us, length us, event | category | flops | bytes accessed | tf_op | source)
XLA Modules:
  0.0 469.4 jit_solution(14942132019180498987)
XLA Ops:
  20.4 32.4 %all-gather.8.cloned.1.call-done = f32[8,34,1536]{2,1,0:T(8,128)} async-done(((f32[1,34,1536]{2,1,0:T(8,128)}), f32[8,34,1536]{2,1,0:T(8,128)}) %all-gather.8.cloned.1.call-update) | async-done | bytes 1671184 | tf_op jit(solution)/shard_map/all_gather | solution.py:24
  58.0 4.0 multiply_reduce_fusion.7
  64.0 7.3 %all-to-all-start = ((f32[16,2,1536]{2,1,0:T(2,128)}), f32[16,2,1536]{2,1,0:T(2,128)S(1)}, u32[]{:S(2)}, u32[]{:S(2)}) async-start(f32[16,2,1536]{2,1,0:T(2,128)} %broadcast_in_dim.18), calls=%async_computation | async-start | bytes 393216 | tf_op jit(solution)/shard_map/all_to_all | solution.py:53
  73.8 4.3 all-to-all-done
  79.1 135.3 %all-gather.6.cloned.1.call-done = bf16[1,12288,1536]{2,1,0:T(8,128)(2,1)} async-done(((bf16[1,48,1536]{2,1,0:T(8,128)(2,1)}), bf16[1,12288,1536]{2,1,0:T(8,128)(2,1)}) %all-gather.6.cloned.1.call-update) | async-done | bytes 37748752 | tf_op jit(solution)/shard_map/all_gather | solution.py:21
  227.8 3.9 multiply_reduce_fusion.6
  233.7 8.7 %all-to-all-start.1 = ((f32[16,2,1536]{2,1,0:T(2,128)}), f32[16,2,1536]{2,1,0:T(2,128)S(1)}, u32[]{:S(2)}, u32[]{:S(2)}) async-start(f32[16,2,1536]{2,1,0:T(2,128)} %broadcast_in_dim.19), calls=%async_computation.1 | async-start | bytes 393216 | tf_op jit(solution)/shard_map/all_to_all | solution.py:53
  244.4 5.0 %all-to-all-done.1 = f32[16,2,1536]{2,1,0:T(2,128)S(1)} async-done(((f32[16,2,1536]{2,1,0:T(2,128)}), f32[16,2,1536]{2,1,0:T(2,128)S(1)}, u32[]{:S(2)}, u32[]{:S(2)}) %all-to-all-start.1) | async-done | bytes 196640 | tf_op jit(solution)/shard_map/all_to_all | solution.py:53
  262.9 3.9 multiply_reduce_fusion.5
  269.0 8.6 %all-to-all-start.2 = ((f32[16,2,1536]{2,1,0:T(2,128)}), f32[16,2,1536]{2,1,0:T(2,128)S(1)}, u32[]{:S(2)}, u32[]{:S(2)}) async-start(f32[16,2,1536]{2,1,0:T(2,128)} %broadcast_in_dim.20), calls=%async_computation.2 | async-start | bytes 393216 | tf_op jit(solution)/shard_map/all_to_all | solution.py:53
  279.5 4.9 %all-to-all-done.2 = f32[16,2,1536]{2,1,0:T(2,128)S(1)} async-done(((f32[16,2,1536]{2,1,0:T(2,128)}), f32[16,2,1536]{2,1,0:T(2,128)S(1)}, u32[]{:S(2)}, u32[]{:S(2)}) %all-to-all-start.2) | async-done | bytes 196640 | tf_op jit(solution)/shard_map/all_to_all | solution.py:53
  298.1 3.9 multiply_reduce_fusion.4
  304.0 8.6 %all-to-all-start.3 = ((f32[16,2,1536]{2,1,0:T(2,128)}), f32[16,2,1536]{2,1,0:T(2,128)S(1)}, u32[]{:S(2)}, u32[]{:S(2)}) async-start(f32[16,2,1536]{2,1,0:T(2,128)} %broadcast_in_dim.21), calls=%async_computation.3 | async-start | bytes 393216 | tf_op jit(solution)/shard_map/all_to_all | solution.py:53
  314.7 4.7 %all-to-all-done.3 = f32[16,2,1536]{2,1,0:T(2,128)S(1)} async-done(((f32[16,2,1536]{2,1,0:T(2,128)}), f32[16,2,1536]{2,1,0:T(2,128)S(1)}, u32[]{:S(2)}, u32[]{:S(2)}) %all-to-all-start.3) | async-done | bytes 196640 | tf_op jit(solution)/shard_map/all_to_all | solution.py:53
  333.1 3.9 multiply_reduce_fusion.3
  339.0 8.6 %all-to-all-start.4 = ((f32[16,2,1536]{2,1,0:T(2,128)}), f32[16,2,1536]{2,1,0:T(2,128)S(1)}, u32[]{:S(2)}, u32[]{:S(2)}) async-start(f32[16,2,1536]{2,1,0:T(2,128)} %broadcast_in_dim.22), calls=%async_computation.4 | async-start | bytes 393216 | tf_op jit(solution)/shard_map/all_to_all | solution.py:53
  349.5 5.0 %all-to-all-done.4 = f32[16,2,1536]{2,1,0:T(2,128)S(1)} async-done(((f32[16,2,1536]{2,1,0:T(2,128)}), f32[16,2,1536]{2,1,0:T(2,128)S(1)}, u32[]{:S(2)}, u32[]{:S(2)}) %all-to-all-start.4) | async-done | bytes 196640 | tf_op jit(solution)/shard_map/all_to_all | solution.py:53
  368.0 3.9 multiply_reduce_fusion.2
  374.0 8.6 %all-to-all-start.5 = ((f32[16,2,1536]{2,1,0:T(2,128)}), f32[16,2,1536]{2,1,0:T(2,128)S(1)}, u32[]{:S(2)}, u32[]{:S(2)}) async-start(f32[16,2,1536]{2,1,0:T(2,128)} %broadcast_in_dim.23), calls=%async_computation.5 | async-start | bytes 393216 | tf_op jit(solution)/shard_map/all_to_all | solution.py:53
  384.3 5.2 %all-to-all-done.5 = f32[16,2,1536]{2,1,0:T(2,128)S(1)} async-done(((f32[16,2,1536]{2,1,0:T(2,128)}), f32[16,2,1536]{2,1,0:T(2,128)S(1)}, u32[]{:S(2)}, u32[]{:S(2)}) %all-to-all-start.5) | async-done | bytes 196640 | tf_op jit(solution)/shard_map/all_to_all | solution.py:53
  408.3 15.3 %all_to_all.40 = f32[16,2,1536]{2,1,0:T(2,128)S(1)} all-to-all(f32[16,2,1536]{2,1,0:T(2,128)S(1)} %broadcast_in_dim.24), channel_id=1, replica_groups=mesh['segment'=8,'ctx'=16,'dp'=2] {'ctx'}, dimensions={0} | all-to-all | bytes 393216 | tf_op jit(solution)/shard_map/all_to_all | solution.py:53
  437.1 3.9 multiply_reduce_fusion
  442.4 15.2 %all_to_all.41 = f32[16,2,1536]{2,1,0:T(2,128)S(1)} all-to-all(f32[16,2,1536]{2,1,0:T(2,128)S(1)} %broadcast_in_dim.25), channel_id=1, replica_groups=mesh['segment'=8,'ctx'=16,'dp'=2] {'ctx'}, dimensions={0} | all-to-all | bytes 393216 | tf_op jit(solution)/shard_map/all_to_all | solution.py:53
  458.6 4.0 fusion.31
  (180 shorter events, 145.1 us)
Async XLA Ops:
  6.5 46.3 %all-gather.8.cloned.1.call-start = ((), (), s32[]{:S(2)}) async-start(), calls=%async_computation.9 | async-start | bytes 2211840 | tf_op jit(solution)/shard_map/all_gather | solution.py:24
  8.3 206.2 %all-gather.6.cloned.1.call-start = ((), (), s32[]{:S(2)}) async-start(), calls=%async_computation.8 | async-start | bytes 37896192 | tf_op jit(solution)/shard_map/all_gather | solution.py:21
  14.6 43.4 %collective-permute-start = (bf16[16,1536]{1,0:T(8,128)(2,1)S(1)}, bf16[16,1536]{1,0:T(8,128)(2,1)S(1)}, u32[]{:S(2)}, u32[]{:S(2)}) collective-permute-start(bf16[16,1536]{1,0:T(8,128)(2,1)S(1)} %get-tuple-element.323), channel_id=1, source_target_pairs={{0,2},{2,4},{4,6},{6,8},{8,10},{10,12},{12,14},{14,16},{16,18},{18... | collective-permute-start | bytes 147464 | tf_op jit(solution)/shard_map/ppermute | solution.py:44
  18.1 39.9 %collective-permute-start.1 = (bf16[16,1536]{1,0:T(8,128)(2,1)S(1)}, bf16[16,1536]{1,0:T(8,128)(2,1)S(1)}, u32[]{:S(2)}, u32[]{:S(2)}) collective-permute-start(bf16[16,1536]{1,0:T(8,128)(2,1)S(1)} %get-tuple-element.324), channel_id=1, source_target_pairs={{2,0},{4,2},{6,4},{8,6},{10,8},{12,10},{14,12},{16,14},{18,16},{20... | collective-permute-start | bytes 147464 | tf_op jit(solution)/shard_map/ppermute | solution.py:45
  64.0 14.2 %all-to-all-start = ((f32[16,2,1536]{2,1,0:T(2,128)}), f32[16,2,1536]{2,1,0:T(2,128)S(1)}, u32[]{:S(2)}, u32[]{:S(2)}) async-start(f32[16,2,1536]{2,1,0:T(2,128)} %broadcast_in_dim.18), calls=%async_computation | async-start | bytes 393216 | tf_op jit(solution)/shard_map/all_to_all | solution.py:53
  218.4 7.7 %collective-permute-start.4 = (bf16[16,1536]{1,0:T(8,128)(2,1)S(1)}, bf16[16,1536]{1,0:T(8,128)(2,1)S(1)}, u32[]{:S(2)}, u32[]{:S(2)}) collective-permute-start(bf16[16,1536]{1,0:T(8,128)(2,1)S(1)} %get-tuple-element.321), channel_id=1, source_target_pairs={{0,2},{2,4},{4,6},{6,8},{8,10},{10,12},{12,14},{14,16},{16,18},{18... | collective-permute-start | bytes 147464 | tf_op jit(solution)/shard_map/ppermute | solution.py:44
  221.8 6.0 %collective-permute-start.5 = (bf16[16,1536]{1,0:T(8,128)(2,1)S(1)}, bf16[16,1536]{1,0:T(8,128)(2,1)S(1)}, u32[]{:S(2)}, u32[]{:S(2)}) collective-permute-start(bf16[16,1536]{1,0:T(8,128)(2,1)S(1)} %get-tuple-element.322), channel_id=1, source_target_pairs={{2,0},{4,2},{6,4},{8,6},{10,8},{12,10},{14,12},{16,14},{18,16},{20... | collective-permute-start | bytes 147464 | tf_op jit(solution)/shard_map/ppermute | solution.py:45
  233.7 15.6 %all-to-all-start.1 = ((f32[16,2,1536]{2,1,0:T(2,128)}), f32[16,2,1536]{2,1,0:T(2,128)S(1)}, u32[]{:S(2)}, u32[]{:S(2)}) async-start(f32[16,2,1536]{2,1,0:T(2,128)} %broadcast_in_dim.19), calls=%async_computation.1 | async-start | bytes 393216 | tf_op jit(solution)/shard_map/all_to_all | solution.py:53
  254.1 7.5 %collective-permute-start.7 = (bf16[16,1536]{1,0:T(8,128)(2,1)S(1)}, bf16[16,1536]{1,0:T(8,128)(2,1)S(1)}, u32[]{:S(2)}, u32[]{:S(2)}) collective-permute-start(bf16[16,1536]{1,0:T(8,128)(2,1)S(1)} %get-tuple-element.319), channel_id=1, source_target_pairs={{0,2},{2,4},{4,6},{6,8},{8,10},{10,12},{12,14},{14,16},{16,18},{18... | collective-permute-start | bytes 147464 | tf_op jit(solution)/shard_map/ppermute | solution.py:44
  256.9 6.0 %collective-permute-start.8 = (bf16[16,1536]{1,0:T(8,128)(2,1)S(1)}, bf16[16,1536]{1,0:T(8,128)(2,1)S(1)}, u32[]{:S(2)}, u32[]{:S(2)}) collective-permute-start(bf16[16,1536]{1,0:T(8,128)(2,1)S(1)} %get-tuple-element.320), channel_id=1, source_target_pairs={{2,0},{4,2},{6,4},{8,6},{10,8},{12,10},{14,12},{16,14},{18,16},{20... | collective-permute-start | bytes 147464 | tf_op jit(solution)/shard_map/ppermute | solution.py:45
  269.0 15.5 %all-to-all-start.2 = ((f32[16,2,1536]{2,1,0:T(2,128)}), f32[16,2,1536]{2,1,0:T(2,128)S(1)}, u32[]{:S(2)}, u32[]{:S(2)}) async-start(f32[16,2,1536]{2,1,0:T(2,128)} %broadcast_in_dim.20), calls=%async_computation.2 | async-start | bytes 393216 | tf_op jit(solution)/shard_map/all_to_all | solution.py:53
  289.3 7.3 %collective-permute-start.10 = (bf16[16,1536]{1,0:T(8,128)(2,1)S(1)}, bf16[16,1536]{1,0:T(8,128)(2,1)S(1)}, u32[]{:S(2)}, u32[]{:S(2)}) collective-permute-start(bf16[16,1536]{1,0:T(8,128)(2,1)S(1)} %get-tuple-element.317), channel_id=1, source_target_pairs={{0,2},{2,4},{4,6},{6,8},{8,10},{10,12},{12,14},{14,16},{16,18},{18... | collective-permute-start | bytes 147464 | tf_op jit(solution)/shard_map/ppermute | solution.py:44
  292.1 6.0 %collective-permute-start.11 = (bf16[16,1536]{1,0:T(8,128)(2,1)S(1)}, bf16[16,1536]{1,0:T(8,128)(2,1)S(1)}, u32[]{:S(2)}, u32[]{:S(2)}) collective-permute-start(bf16[16,1536]{1,0:T(8,128)(2,1)S(1)} %get-tuple-element.318), channel_id=1, source_target_pairs={{2,0},{4,2},{6,4},{8,6},{10,8},{12,10},{14,12},{16,14},{18,16},{20... | collective-permute-start | bytes 147464 | tf_op jit(solution)/shard_map/ppermute | solution.py:45
  304.0 15.5 %all-to-all-start.3 = ((f32[16,2,1536]{2,1,0:T(2,128)}), f32[16,2,1536]{2,1,0:T(2,128)S(1)}, u32[]{:S(2)}, u32[]{:S(2)}) async-start(f32[16,2,1536]{2,1,0:T(2,128)} %broadcast_in_dim.21), calls=%async_computation.3 | async-start | bytes 393216 | tf_op jit(solution)/shard_map/all_to_all | solution.py:53
  324.3 7.8 %collective-permute-start.13 = (bf16[16,1536]{1,0:T(8,128)(2,1)S(1)}, bf16[16,1536]{1,0:T(8,128)(2,1)S(1)}, u32[]{:S(2)}, u32[]{:S(2)}) collective-permute-start(bf16[16,1536]{1,0:T(8,128)(2,1)S(1)} %get-tuple-element.315), channel_id=1, source_target_pairs={{0,2},{2,4},{4,6},{6,8},{8,10},{10,12},{12,14},{14,16},{16,18},{18... | collective-permute-start | bytes 147464 | tf_op jit(solution)/shard_map/ppermute | solution.py:44
  327.1 6.0 %collective-permute-start.14 = (bf16[16,1536]{1,0:T(8,128)(2,1)S(1)}, bf16[16,1536]{1,0:T(8,128)(2,1)S(1)}, u32[]{:S(2)}, u32[]{:S(2)}) collective-permute-start(bf16[16,1536]{1,0:T(8,128)(2,1)S(1)} %get-tuple-element.316), channel_id=1, source_target_pairs={{2,0},{4,2},{6,4},{8,6},{10,8},{12,10},{14,12},{16,14},{18,16},{20... | collective-permute-start | bytes 147464 | tf_op jit(solution)/shard_map/ppermute | solution.py:45
  339.0 15.5 %all-to-all-start.4 = ((f32[16,2,1536]{2,1,0:T(2,128)}), f32[16,2,1536]{2,1,0:T(2,128)S(1)}, u32[]{:S(2)}, u32[]{:S(2)}) async-start(f32[16,2,1536]{2,1,0:T(2,128)} %broadcast_in_dim.22), calls=%async_computation.4 | async-start | bytes 393216 | tf_op jit(solution)/shard_map/all_to_all | solution.py:53
  359.3 7.7 %collective-permute-start.16 = (bf16[16,1536]{1,0:T(8,128)(2,1)S(1)}, bf16[16,1536]{1,0:T(8,128)(2,1)S(1)}, u32[]{:S(2)}, u32[]{:S(2)}) collective-permute-start(bf16[16,1536]{1,0:T(8,128)(2,1)S(1)} %get-tuple-element.313), channel_id=1, source_target_pairs={{0,2},{2,4},{4,6},{6,8},{8,10},{10,12},{12,14},{14,16},{16,18},{18... | collective-permute-start | bytes 147464 | tf_op jit(solution)/shard_map/ppermute | solution.py:44
  362.1 6.0 %collective-permute-start.17 = (bf16[16,1536]{1,0:T(8,128)(2,1)S(1)}, bf16[16,1536]{1,0:T(8,128)(2,1)S(1)}, u32[]{:S(2)}, u32[]{:S(2)}) collective-permute-start(bf16[16,1536]{1,0:T(8,128)(2,1)S(1)} %get-tuple-element.314), channel_id=1, source_target_pairs={{2,0},{4,2},{6,4},{8,6},{10,8},{12,10},{14,12},{16,14},{18,16},{20... | collective-permute-start | bytes 147464 | tf_op jit(solution)/shard_map/ppermute | solution.py:45
  374.0 15.5 %all-to-all-start.5 = ((f32[16,2,1536]{2,1,0:T(2,128)}), f32[16,2,1536]{2,1,0:T(2,128)S(1)}, u32[]{:S(2)}, u32[]{:S(2)}) async-start(f32[16,2,1536]{2,1,0:T(2,128)} %broadcast_in_dim.23), calls=%async_computation.5 | async-start | bytes 393216 | tf_op jit(solution)/shard_map/all_to_all | solution.py:53
  394.3 7.7 %collective-permute-start.19 = (bf16[16,1536]{1,0:T(8,128)(2,1)S(1)}, bf16[16,1536]{1,0:T(8,128)(2,1)S(1)}, u32[]{:S(2)}, u32[]{:S(2)}) collective-permute-start(bf16[16,1536]{1,0:T(8,128)(2,1)S(1)} %get-tuple-element.311), channel_id=1, source_target_pairs={{0,2},{2,4},{4,6},{6,8},{8,10},{10,12},{12,14},{14,16},{16,18},{18... | collective-permute-start | bytes 147464 | tf_op jit(solution)/shard_map/ppermute | solution.py:44
  397.0 6.0 %collective-permute-start.20 = (bf16[16,1536]{1,0:T(8,128)(2,1)S(1)}, bf16[16,1536]{1,0:T(8,128)(2,1)S(1)}, u32[]{:S(2)}, u32[]{:S(2)}) collective-permute-start(bf16[16,1536]{1,0:T(8,128)(2,1)S(1)} %get-tuple-element.312), channel_id=1, source_target_pairs={{2,0},{4,2},{6,4},{8,6},{10,8},{12,10},{14,12},{16,14},{18,16},{20... | collective-permute-start | bytes 147464 | tf_op jit(solution)/shard_map/ppermute | solution.py:45
  428.4 7.6 %collective-permute-start.22 = (bf16[16,1536]{1,0:T(8,128)(2,1)S(1)}, bf16[16,1536]{1,0:T(8,128)(2,1)S(1)}, u32[]{:S(2)}, u32[]{:S(2)}) collective-permute-start(bf16[16,1536]{1,0:T(8,128)(2,1)S(1)} %get-tuple-element.309), channel_id=1, source_target_pairs={{0,2},{2,4},{4,6},{6,8},{8,10},{10,12},{12,14},{14,16},{16,18},{18... | collective-permute-start | bytes 147464 | tf_op jit(solution)/shard_map/ppermute | solution.py:44
  431.2 6.0 %collective-permute-start.23 = (bf16[16,1536]{1,0:T(8,128)(2,1)S(1)}, bf16[16,1536]{1,0:T(8,128)(2,1)S(1)}, u32[]{:S(2)}, u32[]{:S(2)}) collective-permute-start(bf16[16,1536]{1,0:T(8,128)(2,1)S(1)} %get-tuple-element.310), channel_id=1, source_target_pairs={{2,0},{4,2},{6,4},{8,6},{10,8},{12,10},{14,12},{16,14},{18,16},{20... | collective-permute-start | bytes 147464 | tf_op jit(solution)/shard_map/ppermute | solution.py:45
  (10 other events, 13.5 us)
Sparse Core Ops, SparseCore 0:
  9.1 43.6 all-gather.7
  56.7 157.7 all-gather.5

commit v2 on v1

v2 whole, which is shorter than its diff:
```python
import functools
import jax
import jax.numpy as jnp
from jax import lax
from jax.experimental import pallas as pl
from jax.experimental.pallas import tpu as pltpu
from jax.sharding import PartitionSpec as P

EPSILON = 1e-05
LANES = 128


def module_kernel(do_mm, do_conv, rim, taps_n, chunks, w_row, *refs):
    refs = list(refs)
    scal = refs.pop(0)
    if do_mm:
        mixed, low, high = refs.pop(0), refs.pop(0), refs.pop(0)
        sums = refs.pop(0)
        gain_bias, w_hbm = refs.pop(0), refs.pop(0)
    state = refs.pop(0)
    if do_conv:
        taps = refs.pop(0)
    state_out = refs.pop(0)
    if do_conv:
        mixed_out, sums_out, edge_low, edge_high = [refs.pop(0) for _ in range(4)]
    if do_mm:
        act_s, w_s, sems = refs.pop(0), refs.pop(0), refs.pop(0)
    if do_conv:
        norm_s, mask_s = refs.pop(0), refs.pop(0)

    ext, width = state.shape
    own = ext - 2 * rim
    length = scal[0]
    first = scal[1]
    lane_groups = width // LANES

    def row_valid(row, rows, lanes):
        at = lax.broadcasted_iota(jnp.int32, (rows, lanes), 0) + (first + row)
        return jnp.where((at >= 0) & (at < length), 1.0, 0.0).astype(jnp.float32)

    if do_mm:
        wide = width // chunks
        copies = []
        for n in range(chunks):
            lanes = pl.ds(n * wide, wide)
            copies.append(
                pltpu.make_async_copy(
                    w_hbm.at[pl.ds(w_row, width), lanes], w_s.at[:, lanes], sems.at[n]
                )
            )
            copies[-1].start()
        total = sums[0]
        for s in range(1, sums.shape[0]):
            total = total + sums[s]
        count = scal[2].astype(jnp.float32)
        mean = total[0:1] / count
        var = total[1:2] / count - mean * mean
        scale = lax.rsqrt(var + EPSILON) * gain_bias[0:1]
        shift = gain_bias[1:2] - mean * scale
        scale, shift = 0.5 * scale, 0.5 * shift

        for g in range(lane_groups):
            lanes = slice(g * LANES, (g + 1) * LANES)
            sc, sh = scale[:, lanes], shift[:, lanes]
            for src, row, rows in ((low, 0, rim), (mixed, rim, own), (high, rim + own, rim)):
                half = src[:, lanes].astype(jnp.float32) * sc + sh
                act = (half + half * jnp.tanh(half)) * row_valid(row, rows, LANES)
                act_s[row : row + rows, lanes] = act.astype(jnp.bfloat16)
        top = 0 if do_conv else rim
        rows = ext if do_conv else own
        for n in range(chunks):
            lanes = slice(n * wide, (n + 1) * wide)
            copies[n].wait()
            product = jnp.dot(
                act_s[top : top + rows, :], w_s[:, lanes], preferred_element_type=jnp.float32
            )
            old = state[top : top + rows, lanes].astype(jnp.float32)
            state_out[:, lanes] = (old + product).astype(jnp.bfloat16)
    elif do_conv:
        state_out[...] = state[...]

    if do_conv:
        block = 16

        def norm_rows(i, carry):
            row = pl.multiple_of(i * block, block)
            x = state_out[pl.ds(row, block), :].astype(jnp.float32)
            mean = jnp.mean(x, axis=1, keepdims=True)
            x = x - mean
            var = jnp.mean(x * x, axis=1, keepdims=True)
            y = x * (lax.rsqrt(var + EPSILON) * row_valid(row, block, 1))
            norm_s[pl.ds(row, block), :] = y.astype(jnp.bfloat16).astype(jnp.float32)
            return carry

        lax.fori_loop(0, ext // block, norm_rows, 0)
        mask_s[...] = row_valid(rim, own, LANES)

        def conv_lanes(g, carry):
            lanes = pl.ds(pl.multiple_of(g * LANES, LANES), LANES)
            tap = [jnp.broadcast_to(taps[k : k + 1, lanes], (8, LANES)) for k in range(taps_n)]
            tiles = own // 8
            acc = [None] * tiles
            for at in range(8 * (tiles - 1) + taps_n):
                v = norm_s[pl.ds(at, 8), lanes]
                for i in range(tiles):
                    k = at - 8 * i
                    if 0 <= k < taps_n:
                        term = tap[k] * v
                        acc[i] = term if acc[i] is None else acc[i] + term
            one = two = None
            for i in range(tiles):
                mixed_out[8 * i : 8 * i + 8, lanes] = acc[i]
                m = acc[i] * mask_s[8 * i : 8 * i + 8, :]
                q = m * acc[i]
                one = m if one is None else one + m
                two = q if two is None else two + q
            sums_out[0:1, lanes] = jnp.sum(one, axis=0, keepdims=True)
            sums_out[1:2, lanes] = jnp.sum(two, axis=0, keepdims=True)
            edge_low[:, lanes] = mixed_out[0:rim, lanes].astype(jnp.bfloat16)
            edge_high[:, lanes] = mixed_out[own - rim : own, lanes].astype(jnp.bfloat16)
            return carry

        lax.fori_loop(0, lane_groups, conv_lanes, 0)


def run_module(scal, state, prev=None, taps=None, w_row=0):
    ext, width = state.shape
    rim = 16
    own = ext - 2 * rim
    chunks = 6
    do_mm, do_conv = prev is not None, taps is not None
    vmem = pl.BlockSpec(memory_space=pltpu.VMEM)
    args, specs = [scal], [pl.BlockSpec(memory_space=pltpu.SMEM)]
    scratch = []
    if do_mm:
        mixed, low, high, sums, gain_bias, w = prev
        args += [mixed, low, high, sums, gain_bias]
        specs += [vmem] * 5
        args.append(w)
        specs.append(pl.BlockSpec(memory_space=pl.ANY))
        scratch += [
            pltpu.VMEM((ext, width), jnp.bfloat16),
            pltpu.VMEM((width, width), jnp.bfloat16),
            pltpu.SemaphoreType.DMA((chunks,)),
        ]
    args.append(state)
    specs.append(vmem)
    taps_n = 0
    if do_conv:
        taps_n = taps.shape[0]
        args.append(taps)
        specs.append(vmem)
        scratch += [pltpu.VMEM((ext, width), jnp.float32), pltpu.VMEM((own, LANES), jnp.float32)]
        shapes = [
            jax.ShapeDtypeStruct((ext, width), jnp.bfloat16),
            jax.ShapeDtypeStruct((own, width), jnp.float32),
            jax.ShapeDtypeStruct((2, width), jnp.float32),
            jax.ShapeDtypeStruct((rim, width), jnp.bfloat16),
            jax.ShapeDtypeStruct((rim, width), jnp.bfloat16),
        ]
    else:
        shapes = [jax.ShapeDtypeStruct((own, width), jnp.bfloat16)]
    return pl.pallas_call(
        functools.partial(module_kernel, do_mm, do_conv, rim, taps_n, chunks, w_row),
        out_shape=shapes,
        in_specs=specs,
        out_specs=[vmem] * len(shapes),
        scratch_shapes=scratch,
        compiler_params=pltpu.CompilerParams(vmem_limit_bytes=24 << 20),
        name="module_step",
    )(*args)


def shards(frames_in, lengths, depth_kernel, batch_gain, batch_bias, out_weight):
    layer_total = lax.axis_size("segment")
    ctx_count = lax.axis_size("ctx")
    segment_index = lax.axis_index("segment")
    ctx_index = lax.axis_index("ctx")
    dp_index = lax.axis_index("dp")
    frames_dev = frames_in.shape[2]
    width = frames_in.shape[3]
    kernel_size = depth_kernel.shape[1]
    rim = kernel_size // 2
    both = [(0, 1), (1, 0)]
    forward = [(i, i + 1) for i in range(ctx_count - 1)]
    backward = [(b, a) for a, b in forward]

    half_rows = out_weight.shape[1] // 2
    mine = lax.dynamic_slice_in_dim(out_weight[0], dp_index * half_rows, half_rows, 0)
    weights = lax.all_gather(mine, ("segment", "ctx", "dp"), axis=0, tiled=True)
    params = jnp.concatenate([depth_kernel[0], batch_gain, batch_bias], axis=0)
    params = lax.all_gather(params, "segment", axis=0)

    mine_len = lax.dynamic_slice_in_dim(lengths[0], segment_index, 1, 0)
    count = mine_len + lax.ppermute(mine_len, "dp", both)
    first = (ctx_index * frames_dev - rim).astype(jnp.int32)
    scal = jnp.concatenate([mine_len, first[None], count])

    def around(to_low, to_high):
        low = lax.ppermute(to_high, "ctx", forward)
        high = lax.ppermute(to_low, "ctx", backward)
        return low, high

    own = lax.dynamic_index_in_dim(frames_in[0], segment_index, 0, keepdims=False)
    low, high = around(own[:rim], own[frames_dev - rim :])
    state = jnp.concatenate([low, own, high], axis=0)

    prev = None
    for layer in range(layer_total):
        taps = params[layer, :kernel_size]
        state, mixed, sums, edge_low, edge_high = run_module(
            scal, state, prev, taps, (layer - 1) * width
        )
        low, high = around(edge_low, edge_high)
        sums = sums + lax.ppermute(sums, "dp", both)
        sums = lax.all_to_all(
            jnp.broadcast_to(sums[None], (ctx_count, *sums.shape)), "ctx", 0, 0, tiled=True
        )
        gain_bias = params[layer, kernel_size:]
        prev = (mixed, low, high, sums, gain_bias, weights)
    (state,) = run_module(scal, state, prev, None, (layer_total - 1) * width)
    return state[None, None]


def solution(mesh):
    placed = (
        P("dp", None, "ctx", None),
        P("dp", None),
        P("segment", None, None),
        P("segment", None),
        P("segment", None),
        P("segment", "ctx", None),
    )
    return jax.shard_map(
        shards,
        mesh=mesh,
        in_specs=placed,
        out_specs=P("dp", "segment", "ctx", None),
        check_vma=False,
    )
```

time: 474 us -> 456 us (0.962)
  Pallas kernels: 0 us -> 88.9 us
  other arithmetic: 48.5 us -> 2.53 us
  blocking collectives: 30.5 us -> 0 us
  matrix products: 27.3 us -> 0 us
  starting transfers between devices: 98.3 us -> 119 us
  waiting for transfers between devices: 216 us -> 202 us
  local copies, waits for them, and re-layouts: 33.1 us -> 25.1 us
    pallas_call x0 -> x9, Pallas kernels: none -> 88.9 us  [run_module(): pl.pallas_call(functools.partial(module_kernel, do_mm, do_conv, rim, taps...]
    reduce_sum x25 -> x0, other arithmetic: 35.6 us -> none  [the longest x8 31 us: shards(): sums = jnp.stack([jnp.sum(masked, axis=0), jnp.sum(masked * mixed, axis=0)])]
    all_to_all x2 -> x0, blocking collectives: 30.5 us -> none  [shards(): lax.all_to_all(jnp.broadcast_to(sums[None], (ctx_count, *sums.shape)), 'c...]
    dot_general x8 -> x0, matrix products: 27.3 us -> none  [shards(): jnp.dot(activation, weights[layer], preferred_element_type=jnp.float32)]
    slice x23 -> x1, local copies, waits for them, and re-layouts: 26.7 us -> 0.83 us  [shards(): low, high = around(own[:rim], own[frames_dev - rim:])]
    all_to_all x6 -> x8, waiting for transfers between devices: 29.1 us -> 5.72 us  [shards(): lax.all_to_all(jnp.broadcast_to(sums[None], (ctx_count, *sums.shape)), 'c...]
    all_to_all x6 -> x8, starting transfers between devices: 50.4 us -> 65.5 us  [shards(): lax.all_to_all(jnp.broadcast_to(sums[None], (ctx_count, *sums.shape)), 'c...]
    ppermute x17 -> x19, waiting for transfers between devices: 9.94 us -> 24.9 us  [the longest x9 23.3 us: around(): high = lax.ppermute(to_low, 'ctx', backward)]
  transfers between devices with their start and end apart: 33 -> 37, of which waited for: 24 -> 25; matrix products, arithmetic and copies ran while one was open for 8% -> 2% of each run, Pallas kernels for 0% -> 2%
where the time goes in v2:
time: 456 us; the launch traced here: 452 us
  waiting for transfers between devices  202 us (44%)
  starting transfers between devices  119 us (26%)
  Pallas kernels  88.9 us (19%)
  local copies, waits for them, and re-layouts  25.1 us (6%)
  between operations  15.1 us (3%)
    all_gather x1, waiting for transfers between devices, shards(): weights = lax.all_gather(mine, ('segment', 'ctx', 'dp'), axis=0, tiled=True)  131 us
    pallas_call x9, Pallas kernels, run_module(): pl.pallas_call(functools.partial(module_kernel, do_mm, do_conv, rim, taps...  88.9 us
    all_to_all x8, starting transfers between devices, shards(): lax.all_to_all(jnp.broadcast_to(sums[None], (ctx_count, *sums.shape)), 'c...  65.5 us
    all_gather x1, waiting for transfers between devices, shards(): params = lax.all_gather(params, 'segment', axis=0)  32.1 us
    ppermute x9, starting transfers between devices, around(): low = lax.ppermute(to_high, 'ctx', forward)  30.4 us
    ppermute x9, waiting for transfers between devices, around(): high = lax.ppermute(to_low, 'ctx', backward)  23.3 us
    ppermute x9, starting transfers between devices, around(): high = lax.ppermute(to_low, 'ctx', backward)  22.3 us
    unnamed x30, local copies, waits for them, and re-layouts  12.8 us
  transfers between devices with their start and end apart: 37, of which 25 were waited for; matrix products, arithmetic and copies ran while one was open for 2% of the time, Pallas kernels for 2%

profile of v2, /device:TPU:8, one launch (start us, length us, event | category | flops | bytes accessed | tf_op | source)
XLA Modules:
  0.0 452.2 jit_solution(12094077840868765010)
XLA Ops:
  11.2 3.5 collective-permute-start.1
  20.7 32.1 %all-gather.8.cloned.1.call-done = f32[8,34,1536]{2,1,0:T(8,128)} async-done(((f32[1,34,1536]{2,1,0:T(8,128)}), f32[8,34,1536]{2,1,0:T(8,128)}) %all-gather.8.cloned.1.call-update) | async-done | bytes 1671184 | tf_op jit(solution)/shard_map/all_gather | solution.py:192
  54.4 8.0 %module_step.9 = (bf16[160,1536]{1,0:T(8,128)(2,1)S(1)}, f32[128,1536]{1,0:T(8,128)S(1)}, f32[2,1536]{1,0:T(2,128)S(1)}, bf16[16,1536]{1,0:T(8,128)(2,1)}, bf16[16,1536]{1,0:T(8,128)(2,1)}) custom-call(s32[3]{0:T(128)S(1)} %pad_add_fusion.refs_0_, bf16[160,1536]{1,0:T(8,128)(2,1)S(1)} %pad_maximum_fusion.refs_1_, f32[32,1536]{1,0:T(8,128)S(1)} %get-tuple-element.102.refs_2_), custom_call_target="tpu_custom_call" | custom-call | tf_op jit(solution)/shard_map/module_step/pallas_call | solution.py:163
  62.4 3.4 collective-permute-start.3
  69.0 7.3 %all-to-all-start = ((f32[16,2,1536]{2,1,0:T(2,128)}), f32[16,2,1536]{2,1,0:T(2,128)S(1)}, u32[]{:S(2)}, u32[]{:S(2)}) async-start(f32[16,2,1536]{2,1,0:T(2,128)} %broadcast_in_dim.21), calls=%async_computation | async-start | bytes 393216 | tf_op jit(solution)/shard_map/all_to_all | solution.py:216
  77.2 5.7 %all-to-all-done.refs_4_ = f32[16,2,1536]{2,1,0:T(2,128)S(1)} async-done(((f32[16,2,1536]{2,1,0:T(2,128)}), f32[16,2,1536]{2,1,0:T(2,128)S(1)}, u32[]{:S(2)}, u32[]{:S(2)}) %all-to-all-start) | async-done | bytes 196640 | tf_op jit(solution)/shard_map/all_to_all | solution.py:216
  82.9 131.3 %all-gather.6.cloned.1.call-done = bf16[1,12288,1536]{2,1,0:T(8,128)(2,1)} async-done(((bf16[1,48,1536]{2,1,0:T(8,128)(2,1)}), bf16[1,12288,1536]{2,1,0:T(8,128)(2,1)}) %all-gather.6.cloned.1.call-update) | async-done | bytes 37748752 | tf_op jit(solution)/shard_map/all_gather | solution.py:190
  214.2 10.9 %module_step.10 = (bf16[160,1536]{1,0:T(8,128)(2,1)S(1)}, f32[128,1536]{1,0:T(8,128)S(1)}, f32[2,1536]{1,0:T(2,128)S(1)}, bf16[16,1536]{1,0:T(8,128)(2,1)S(1)}, bf16[16,1536]{1,0:T(8,128)(2,1)S(1)}) custom-call(s32[3]{0:T(128)S(1)} %pad_add_fusion.refs_0_, f32[128,1536]{1,0:T(8,128)S(1)} %get-tuple-element.45.refs_1_, ...), custom_call_target="tpu_custom_call" | custom-call | tf_op jit(solution)/shard_map/module_step/pallas_call | solution.py:163
  228.7 5.7 %all-to-all-start.1 = ((f32[16,2,1536]{2,1,0:T(2,128)}), f32[16,2,1536]{2,1,0:T(2,128)S(1)}, u32[]{:S(2)}, u32[]{:S(2)}) async-start(f32[16,2,1536]{2,1,0:T(2,128)} %broadcast_in_dim.22), calls=%async_computation.1 | async-start | bytes 393216 | tf_op jit(solution)/shard_map/all_to_all | solution.py:216
  246.0 10.9 %module_step.11 = (bf16[160,1536]{1,0:T(8,128)(2,1)S(1)}, f32[128,1536]{1,0:T(8,128)S(1)}, f32[2,1536]{1,0:T(2,128)S(1)}, bf16[16,1536]{1,0:T(8,128)(2,1)S(1)}, bf16[16,1536]{1,0:T(8,128)(2,1)S(1)}) custom-call(s32[3]{0:T(128)S(1)} %pad_add_fusion.refs_0_, f32[128,1536]{1,0:T(8,128)S(1)} %copy-done.2, bf16[16,1536]{1,0:T(8,128)(2,1)S(1)} %collective-permute-done.6.refs_2_, ...), custom_call_target="tpu_custom_call" | custom-call | tf_op jit(solution)/shard_map/module_step/pallas_call | solution.py:163
  259.6 8.7 %all-to-all-start.2 = ((f32[16,2,1536]{2,1,0:T(2,128)}), f32[16,2,1536]{2,1,0:T(2,128)S(1)}, u32[]{:S(2)}, u32[]{:S(2)}) async-start(f32[16,2,1536]{2,1,0:T(2,128)} %broadcast_in_dim.23), calls=%async_computation.2 | async-start | bytes 393216 | tf_op jit(solution)/shard_map/all_to_all | solution.py:216
  268.3 3.4 collective-permute-start.9
  278.7 10.9 %module_step.12 = (bf16[160,1536]{1,0:T(8,128)(2,1)S(1)}, f32[128,1536]{1,0:T(8,128)S(1)}, f32[2,1536]{1,0:T(2,128)S(1)}, bf16[16,1536]{1,0:T(8,128)(2,1)S(1)}, bf16[16,1536]{1,0:T(8,128)(2,1)S(1)}) custom-call(s32[3]{0:T(128)S(1)} %pad_add_fusion.refs_0_, f32[128,1536]{1,0:T(8,128)S(1)} %get-tuple-element.55.refs_1_, ...), custom_call_target="tpu_custom_call" | custom-call | tf_op jit(solution)/shard_map/module_step/pallas_call | solution.py:163
  292.3 8.7 %all-to-all-start.3 = ((f32[16,2,1536]{2,1,0:T(2,128)}), f32[16,2,1536]{2,1,0:T(2,128)S(1)}, u32[]{:S(2)}, u32[]{:S(2)}) async-start(f32[16,2,1536]{2,1,0:T(2,128)} %broadcast_in_dim.24), calls=%async_computation.3 | async-start | bytes 393216 | tf_op jit(solution)/shard_map/all_to_all | solution.py:216
  301.1 3.4 collective-permute-start.12
  311.5 10.9 %module_step.13 = (bf16[160,1536]{1,0:T(8,128)(2,1)S(1)}, f32[128,1536]{1,0:T(8,128)S(1)}, f32[2,1536]{1,0:T(2,128)S(1)}, bf16[16,1536]{1,0:T(8,128)(2,1)S(1)}, bf16[16,1536]{1,0:T(8,128)(2,1)S(1)}) custom-call(s32[3]{0:T(128)S(1)} %pad_add_fusion.refs_0_, f32[128,1536]{1,0:T(8,128)S(1)} %get-tuple-element.60.refs_1_, ...), custom_call_target="tpu_custom_call" | custom-call | tf_op jit(solution)/shard_map/module_step/pallas_call | solution.py:163
  325.1 8.7 %all-to-all-start.4 = ((f32[16,2,1536]{2,1,0:T(2,128)}), f32[16,2,1536]{2,1,0:T(2,128)S(1)}, u32[]{:S(2)}, u32[]{:S(2)}) async-start(f32[16,2,1536]{2,1,0:T(2,128)} %broadcast_in_dim.25), calls=%async_computation.4 | async-start | bytes 393216 | tf_op jit(solution)/shard_map/all_to_all | solution.py:216
  344.2 10.9 %module_step.14 = (bf16[160,1536]{1,0:T(8,128)(2,1)S(1)}, f32[128,1536]{1,0:T(8,128)S(1)}, f32[2,1536]{1,0:T(2,128)S(1)}, bf16[16,1536]{1,0:T(8,128)(2,1)S(1)}, bf16[16,1536]{1,0:T(8,128)(2,1)S(1)}) custom-call(s32[3]{0:T(128)S(1)} %pad_add_fusion.refs_0_, f32[128,1536]{1,0:T(8,128)S(1)} %get-tuple-element.65.refs_1_, ...), custom_call_target="tpu_custom_call" | custom-call | tf_op jit(solution)/shard_map/module_step/pallas_call | solution.py:163
  357.8 8.7 %all-to-all-start.5 = ((f32[16,2,1536]{2,1,0:T(2,128)}), f32[16,2,1536]{2,1,0:T(2,128)S(1)}, u32[]{:S(2)}, u32[]{:S(2)}) async-start(f32[16,2,1536]{2,1,0:T(2,128)} %broadcast_in_dim.26), calls=%async_computation.5 | async-start | bytes 393216 | tf_op jit(solution)/shard_map/all_to_all | solution.py:216
  377.0 10.9 %module_step.15 = (bf16[160,1536]{1,0:T(8,128)(2,1)S(1)}, f32[128,1536]{1,0:T(8,128)S(1)}, f32[2,1536]{1,0:T(2,128)S(1)}, bf16[16,1536]{1,0:T(8,128)(2,1)S(1)}, bf16[16,1536]{1,0:T(8,128)(2,1)S(1)}) custom-call(s32[3]{0:T(128)S(1)} %pad_add_fusion.refs_0_, f32[128,1536]{1,0:T(8,128)S(1)} %get-tuple-element.70.refs_1_, ...), custom_call_target="tpu_custom_call" | custom-call | tf_op jit(solution)/shard_map/module_step/pallas_call | solution.py:163
  390.6 8.7 %all-to-all-start.6 = ((f32[16,2,1536]{2,1,0:T(2,128)}), f32[16,2,1536]{2,1,0:T(2,128)S(1)}, u32[]{:S(2)}, u32[]{:S(2)}) async-start(f32[16,2,1536]{2,1,0:T(2,128)} %broadcast_in_dim.27), calls=%async_computation.6 | async-start | bytes 393216 | tf_op jit(solution)/shard_map/all_to_all | solution.py:216
  409.7 10.9 %module_step.16 = (bf16[160,1536]{1,0:T(8,128)(2,1)S(1)}, f32[128,1536]{1,0:T(8,128)S(1)}, f32[2,1536]{1,0:T(2,128)S(1)}, bf16[16,1536]{1,0:T(8,128)(2,1)S(1)}, bf16[16,1536]{1,0:T(8,128)(2,1)S(1)}) custom-call(s32[3]{0:T(128)S(1)} %pad_add_fusion.refs_0_, f32[128,1536]{1,0:T(8,128)S(1)} %get-tuple-element.75.refs_1_, ...), custom_call_target="tpu_custom_call" | custom-call | tf_op jit(solution)/shard_map/module_step/pallas_call | solution.py:163
  422.7 8.7 %all-to-all-start.7 = ((f32[16,2,1536]{2,1,0:T(2,128)}), f32[16,2,1536]{2,1,0:T(2,128)S(1)}, u32[]{:S(2)}, u32[]{:S(2)}) async-start(f32[16,2,1536]{2,1,0:T(2,128)} %broadcast_in_dim.28), calls=%async_computation.7 | async-start | bytes 393216 | tf_op jit(solution)/shard_map/all_to_all | solution.py:216
  440.8 4.6 %module_step.17 = bf16[128,1536]{1,0:T(8,128)(2,1)} custom-call(s32[3]{0:T(128)S(1)} %pad_add_fusion.refs_0_, f32[128,1536]{1,0:T(8,128)S(1)} %get-tuple-element.80.refs_1_, bf16[16,1536]{1,0:T(8,128)(2,1)S(1)} %collective-permute-done.24.refs_2_, bf16[16,1536]{1,0:T(8,128)(2,1)S(1)} %collective-permute-done.25.refs_3_, ...), custom_call_target="tpu_custom_call" | custom-call | tf_op jit(solution)/shard_map/module_step/pallas_call | solution.py:163
  (116 shorter events, 100.0 us)
Async XLA Ops:
  6.5 46.3 %all-gather.8.cloned.1.call-start = ((), (), s32[]{:S(2)}) async-start(), calls=%async_computation.9 | async-start | bytes 2211840 | tf_op jit(solution)/shard_map/all_gather | solution.py:192
  8.3 206.0 %all-gather.6.cloned.1.call-start = ((), (), s32[]{:S(2)}) async-start(), calls=%async_computation.8 | async-start | bytes 37896192 | tf_op jit(solution)/shard_map/all_gather | solution.py:190
  10.3 7.7 %collective-permute-start = (s32[1]{0:T(128)}, s32[1]{0:T(128)}, u32[]{:S(2)}, u32[]{:S(2)}) collective-permute-start(s32[1]{0:T(128)} %bitcast), channel_id=1, source_target_pairs={{0,1},{1,0},{2,3},{3,2},{4,5},{5,4},{6,7},{7,6},{8,9},{9,8},{10,11... | collective-permute-start | bytes 20 | tf_op jit(solution)/shard_map/ppermute | solution.py:195
  11.2 8.9 %collective-permute-start.1 = (bf16[16,1536]{1,0:T(8,128)(2,1)S(1)}, bf16[16,1536]{1,0:T(8,128)(2,1)S(1)}, u32[]{:S(2)}, u32[]{:S(2)}) collective-permute-start(bf16[16,1536]{1,0:T(8,128)(2,1)S(1)} %get-tuple-element.85), channel_id=1, source_target_pairs={{0,2},{2,4},{4,6},{6,8},{8,10},{10,12},{12,14},{14,16},{16,18},{18... | collective-permute-start | bytes 147464 | tf_op jit(solution)/shard_map/ppermute | solution.py:200
  62.4 14.9 %collective-permute-start.3 = (bf16[16,1536]{1,0:T(8,128)(2,1)}, bf16[16,1536]{1,0:T(8,128)(2,1)S(1)}, u32[]{:S(2)}, u32[]{:S(2)}) collective-permute-start(bf16[16,1536]{1,0:T(8,128)(2,1)} %get-tuple-element.46), channel_id=1, source_target_pairs={{0,2},{2,4},{4,6},{6,8},{8,10},{10,12},{12,14},{14,16},{16,18},{18... | collective-permute-start | bytes 147464 | tf_op jit(solution)/shard_map/ppermute | solution.py:200
  65.7 11.5 %collective-permute-start.4 = (bf16[16,1536]{1,0:T(8,128)(2,1)}, bf16[16,1536]{1,0:T(8,128)(2,1)S(1)}, u32[]{:S(2)}, u32[]{:S(2)}) collective-permute-start(bf16[16,1536]{1,0:T(8,128)(2,1)} %get-tuple-element.47), channel_id=1, source_target_pairs={{2,0},{4,2},{6,4},{8,6},{10,8},{12,10},{14,12},{16,14},{18,16},{20... | collective-permute-start | bytes 147464 | tf_op jit(solution)/shard_map/ppermute | solution.py:201
  69.0 14.0 %all-to-all-start = ((f32[16,2,1536]{2,1,0:T(2,128)}), f32[16,2,1536]{2,1,0:T(2,128)S(1)}, u32[]{:S(2)}, u32[]{:S(2)}) async-start(f32[16,2,1536]{2,1,0:T(2,128)} %broadcast_in_dim.21), calls=%async_computation | async-start | bytes 393216 | tf_op jit(solution)/shard_map/all_to_all | solution.py:216
  228.7 15.1 %all-to-all-start.1 = ((f32[16,2,1536]{2,1,0:T(2,128)}), f32[16,2,1536]{2,1,0:T(2,128)S(1)}, u32[]{:S(2)}, u32[]{:S(2)}) async-start(f32[16,2,1536]{2,1,0:T(2,128)} %broadcast_in_dim.22), calls=%async_computation.1 | async-start | bytes 393216 | tf_op jit(solution)/shard_map/all_to_all | solution.py:216
  234.5 6.1 %collective-permute-start.6 = (bf16[16,1536]{1,0:T(8,128)(2,1)S(1)}, bf16[16,1536]{1,0:T(8,128)(2,1)S(1)}, u32[]{:S(2)}, u32[]{:S(2)}) collective-permute-start(bf16[16,1536]{1,0:T(8,128)(2,1)S(1)} %get-tuple-element.51), channel_id=1, source_target_pairs={{0,2},{2,4},{4,6},{6,8},{8,10},{10,12},{12,14},{14,16},{16,18},{18... | collective-permute-start | bytes 147464 | tf_op jit(solution)/shard_map/ppermute | solution.py:200
  259.6 18.1 %all-to-all-start.2 = ((f32[16,2,1536]{2,1,0:T(2,128)}), f32[16,2,1536]{2,1,0:T(2,128)S(1)}, u32[]{:S(2)}, u32[]{:S(2)}) async-start(f32[16,2,1536]{2,1,0:T(2,128)} %broadcast_in_dim.23), calls=%async_computation.2 | async-start | bytes 393216 | tf_op jit(solution)/shard_map/all_to_all | solution.py:216
  268.3 6.1 %collective-permute-start.9 = (bf16[16,1536]{1,0:T(8,128)(2,1)S(1)}, bf16[16,1536]{1,0:T(8,128)(2,1)S(1)}, u32[]{:S(2)}, u32[]{:S(2)}) collective-permute-start(bf16[16,1536]{1,0:T(8,128)(2,1)S(1)} %get-tuple-element.56), channel_id=1, source_target_pairs={{0,2},{2,4},{4,6},{6,8},{8,10},{10,12},{12,14},{14,16},{16,18},{18... | collective-permute-start | bytes 147464 | tf_op jit(solution)/shard_map/ppermute | solution.py:200
  271.7 6.0 %collective-permute-start.10 = (bf16[16,1536]{1,0:T(8,128)(2,1)S(1)}, bf16[16,1536]{1,0:T(8,128)(2,1)S(1)}, u32[]{:S(2)}, u32[]{:S(2)}) collective-permute-start(bf16[16,1536]{1,0:T(8,128)(2,1)S(1)} %get-tuple-element.57), channel_id=1, source_target_pairs={{2,0},{4,2},{6,4},{8,6},{10,8},{12,10},{14,12},{16,14},{18,16},{20... | collective-permute-start | bytes 147464 | tf_op jit(solution)/shard_map/ppermute | solution.py:201
  292.3 18.1 %all-to-all-start.3 = ((f32[16,2,1536]{2,1,0:T(2,128)}), f32[16,2,1536]{2,1,0:T(2,128)S(1)}, u32[]{:S(2)}, u32[]{:S(2)}) async-start(f32[16,2,1536]{2,1,0:T(2,128)} %broadcast_in_dim.24), calls=%async_computation.3 | async-start | bytes 393216 | tf_op jit(solution)/shard_map/all_to_all | solution.py:216
  301.1 6.1 %collective-permute-start.12 = (bf16[16,1536]{1,0:T(8,128)(2,1)S(1)}, bf16[16,1536]{1,0:T(8,128)(2,1)S(1)}, u32[]{:S(2)}, u32[]{:S(2)}) collective-permute-start(bf16[16,1536]{1,0:T(8,128)(2,1)S(1)} %get-tuple-element.61), channel_id=1, source_target_pairs={{0,2},{2,4},{4,6},{6,8},{8,10},{10,12},{12,14},{14,16},{16,18},{18... | collective-permute-start | bytes 147464 | tf_op jit(solution)/shard_map/ppermute | solution.py:200
  304.5 6.0 %collective-permute-start.13 = (bf16[16,1536]{1,0:T(8,128)(2,1)S(1)}, bf16[16,1536]{1,0:T(8,128)(2,1)S(1)}, u32[]{:S(2)}, u32[]{:S(2)}) collective-permute-start(bf16[16,1536]{1,0:T(8,128)(2,1)S(1)} %get-tuple-element.62), channel_id=1, source_target_pairs={{2,0},{4,2},{6,4},{8,6},{10,8},{12,10},{14,12},{16,14},{18,16},{20... | collective-permute-start | bytes 147464 | tf_op jit(solution)/shard_map/ppermute | solution.py:201
  325.1 18.1 %all-to-all-start.4 = ((f32[16,2,1536]{2,1,0:T(2,128)}), f32[16,2,1536]{2,1,0:T(2,128)S(1)}, u32[]{:S(2)}, u32[]{:S(2)}) async-start(f32[16,2,1536]{2,1,0:T(2,128)} %broadcast_in_dim.25), calls=%async_computation.4 | async-start | bytes 393216 | tf_op jit(solution)/shard_map/all_to_all | solution.py:216
  333.8 6.1 %collective-permute-start.15 = (bf16[16,1536]{1,0:T(8,128)(2,1)S(1)}, bf16[16,1536]{1,0:T(8,128)(2,1)S(1)}, u32[]{:S(2)}, u32[]{:S(2)}) collective-permute-start(bf16[16,1536]{1,0:T(8,128)(2,1)S(1)} %get-tuple-element.66), channel_id=1, source_target_pairs={{0,2},{2,4},{4,6},{6,8},{8,10},{10,12},{12,14},{14,16},{16,18},{18... | collective-permute-start | bytes 147464 | tf_op jit(solution)/shard_map/ppermute | solution.py:200
  357.8 18.1 %all-to-all-start.5 = ((f32[16,2,1536]{2,1,0:T(2,128)}), f32[16,2,1536]{2,1,0:T(2,128)S(1)}, u32[]{:S(2)}, u32[]{:S(2)}) async-start(f32[16,2,1536]{2,1,0:T(2,128)} %broadcast_in_dim.26), calls=%async_computation.5 | async-start | bytes 393216 | tf_op jit(solution)/shard_map/all_to_all | solution.py:216
  366.6 6.1 %collective-permute-start.18 = (bf16[16,1536]{1,0:T(8,128)(2,1)S(1)}, bf16[16,1536]{1,0:T(8,128)(2,1)S(1)}, u32[]{:S(2)}, u32[]{:S(2)}) collective-permute-start(bf16[16,1536]{1,0:T(8,128)(2,1)S(1)} %get-tuple-element.71), channel_id=1, source_target_pairs={{0,2},{2,4},{4,6},{6,8},{8,10},{10,12},{12,14},{14,16},{16,18},{18... | collective-permute-start | bytes 147464 | tf_op jit(solution)/shard_map/ppermute | solution.py:200
  390.6 18.1 %all-to-all-start.6 = ((f32[16,2,1536]{2,1,0:T(2,128)}), f32[16,2,1536]{2,1,0:T(2,128)S(1)}, u32[]{:S(2)}, u32[]{:S(2)}) async-start(f32[16,2,1536]{2,1,0:T(2,128)} %broadcast_in_dim.27), calls=%async_computation.6 | async-start | bytes 393216 | tf_op jit(solution)/shard_map/all_to_all | solution.py:216
  399.3 6.1 %collective-permute-start.21 = (bf16[16,1536]{1,0:T(8,128)(2,1)S(1)}, bf16[16,1536]{1,0:T(8,128)(2,1)S(1)}, u32[]{:S(2)}, u32[]{:S(2)}) collective-permute-start(bf16[16,1536]{1,0:T(8,128)(2,1)S(1)} %get-tuple-element.76), channel_id=1, source_target_pairs={{0,2},{2,4},{4,6},{6,8},{8,10},{10,12},{12,14},{14,16},{16,18},{18... | collective-permute-start | bytes 147464 | tf_op jit(solution)/shard_map/ppermute | solution.py:200
  402.7 6.0 %collective-permute-start.22 = (bf16[16,1536]{1,0:T(8,128)(2,1)S(1)}, bf16[16,1536]{1,0:T(8,128)(2,1)S(1)}, u32[]{:S(2)}, u32[]{:S(2)}) collective-permute-start(bf16[16,1536]{1,0:T(8,128)(2,1)S(1)} %get-tuple-element.77), channel_id=1, source_target_pairs={{2,0},{4,2},{6,4},{8,6},{10,8},{12,10},{14,12},{16,14},{18,16},{20... | collective-permute-start | bytes 147464 | tf_op jit(solution)/shard_map/ppermute | solution.py:201
  422.7 18.1 %all-to-all-start.7 = ((f32[16,2,1536]{2,1,0:T(2,128)}), f32[16,2,1536]{2,1,0:T(2,128)S(1)}, u32[]{:S(2)}, u32[]{:S(2)}) async-start(f32[16,2,1536]{2,1,0:T(2,128)} %broadcast_in_dim.28), calls=%async_computation.7 | async-start | bytes 393216 | tf_op jit(solution)/shard_map/all_to_all | solution.py:216
  431.4 6.1 %collective-permute-start.24 = (bf16[16,1536]{1,0:T(8,128)(2,1)S(1)}, bf16[16,1536]{1,0:T(8,128)(2,1)S(1)}, u32[]{:S(2)}, u32[]{:S(2)}) collective-permute-start(bf16[16,1536]{1,0:T(8,128)(2,1)S(1)} %get-tuple-element.81), channel_id=1, source_target_pairs={{0,2},{2,4},{4,6},{6,8},{8,10},{10,12},{12,14},{14,16},{16,18},{18... | collective-permute-start | bytes 147464 | tf_op jit(solution)/shard_map/ppermute | solution.py:200
  (28 other events, 58.8 us)
Sparse Core Ops, SparseCore 0:
  9.1 43.6 all-gather.7
  56.7 157.5 all-gather.5
